TPU v7x, 32 devices: a whole 2x2x4 slice. The times are simulated.
32 devices in a mesh: depth: 16 (over z, x, core), band: 2 (over y).
Axes of the slice: x: 2, y: 2, z: 4, core: 2. Of those that a mesh axis runs over, the one named last changes fastest.
Arguments:
- volume: int32 [64, 64, 1024], P('depth', 'band'), may hold values from 0 to 255
- tf_table: int32 [4, 256], replicated, may hold values from 0 to 255
- view_code: int32 [2, 4], replicated, may hold values from -20 to 20
Outputs:
- final_image: float32 [2, 1024, 4, 64], P(None, 'depth', None, 'band')
All inputs are finite; a program needn't handle non-finite values.
Results may differ from a plain program's by a relative error of at most 0.0014.
Values may be sent and summed in bfloat16 or wider, within the bound.
A program may use at most 64 MiB of HBM per device.

v0:
```python
import math
import jax
import jax.numpy as jnp
from jax import lax
from jax.sharding import PartitionSpec as P

VIEWS = 2
MARGIN = 16


def extended(x, sides, width):
    for axis, dim in sides:
        size, length = (lax.axis_size(axis), x.shape[dim])
        up = [(i, (i + 1) % size) for i in range(size - 1)]
        down = [(j, i) for i, j in up]
        last = lax.slice_in_dim(x, length - width, length, axis=dim)
        first = lax.slice_in_dim(x, 0, width, axis=dim)
        before = lax.ppermute(last, axis, up)
        after = lax.ppermute(first, axis, down)
        x = jnp.concatenate([before, x, after], axis=dim)
    return x


def lanczos(offset):
    return jnp.where(jnp.abs(offset) < 3.0, jnp.sinc(offset) * jnp.sinc(offset / 3.0), 0.0)


def split_offset(coefficient, position, length, lift=0):
    numerator = coefficient * (2 * position + 1 - length) + lift * length
    integer_part = numerator // (2 * length)
    fraction = (numerator - integer_part * (2 * length)).astype(jnp.float32) / (2.0 * length)
    return (integer_part, fraction)


def make_palette(tf_table, depth_count):
    table_float = tf_table.astype(jnp.float32)
    opacity = table_float[3] / (64.0 * depth_count)
    premult = table_float[0:3] / 255.0 * opacity
    return jnp.concatenate([premult, opacity[None]], axis=0).astype(jnp.bfloat16)


def classify(codes, palette):
    shape = codes.shape
    last = shape[-1]
    rows = codes.reshape(-1, last)
    row_count = rows.shape[0]
    group_rows = math.gcd(row_count, 8)
    grouped = rows.reshape(row_count // group_rows, group_rows, last)
    table = palette.reshape(4, 16, 16)
    levels = jnp.arange(16, dtype=jnp.int32)

    def lookup(block_codes):
        high_part = block_codes // 16
        low_part = block_codes - high_part * 16
        low_hot = (low_part[None] == levels[:, None, None]).astype(jnp.bfloat16)
        partial_value = jnp.einsum(
            "chl,lgk->chgk", table, low_hot, preferred_element_type=jnp.float32
        )
        high_hot = (high_part[None] == levels[:, None, None]).astype(jnp.float32)
        return jnp.sum(partial_value * high_hot[None], axis=1)

    picked = lax.map(lookup, grouped)
    picked = jnp.transpose(picked, (1, 0, 2, 3)).reshape((4,) + shape)
    return picked.astype(jnp.bfloat16)


def column_weights(integer_part, fraction, block):
    inputs = jnp.arange(3 * block, dtype=jnp.int32)[:, None]
    outputs = jnp.arange(block, dtype=jnp.int32)[None, :]
    distance = inputs - block - outputs - integer_part
    return lanczos(fraction - distance.astype(jnp.float32)).astype(jnp.bfloat16)


def row_weights(integer_part, fraction, out_rows, in_rows, margin):
    outputs = jnp.arange(out_rows, dtype=jnp.int32)[:, None]
    inputs = jnp.arange(in_rows, dtype=jnp.int32)[None, :]
    distance = inputs - margin - outputs - integer_part
    return lanczos(fraction - distance.astype(jnp.float32)).astype(jnp.bfloat16)


def warp_weights(coefficient, first_column, strip_width, margin, total_width):
    columns = first_column + jnp.arange(strip_width, dtype=jnp.int32)
    integer_part, fraction = split_offset(coefficient, columns, total_width, 1)
    inputs = jnp.arange(strip_width + 2 * margin, dtype=jnp.int32)[None, :]
    outputs = jnp.arange(strip_width, dtype=jnp.int32)[:, None]
    distance = inputs - margin - outputs - integer_part[:, None]
    return lanczos(fraction[:, None] - distance.astype(jnp.float32))


def shear_columns(source, tap_matrix, block):
    channels, row_count, extent = source.shape
    blocks = extent // block
    padded = jnp.pad(source, ((0, 0), (0, 0), (block, block)))
    tile_view = padded.reshape(channels, row_count, blocks + 2, block)
    windows = jnp.concatenate(
        [
            tile_view[:, :, 0:blocks],
            tile_view[:, :, 1 : blocks + 1],
            tile_view[:, :, 2 : blocks + 2],
        ],
        axis=3,
    )
    result = jnp.einsum("crbk,kj->bjcr", windows, tap_matrix, preferred_element_type=jnp.float32)
    return result.reshape(extent, channels, row_count).astype(jnp.bfloat16)


def shear_rows(source, tap_matrix):
    return jnp.einsum("xcr,yr->xcy", source, tap_matrix, preferred_element_type=jnp.float32)


def over(front_part, back_part):
    return front_part + (1.0 - front_part[..., 3:4, :]) * back_part


def body(volume, tf_table, view_code):
    slab_count, band_rows, extent = volume.shape
    depth_size = lax.axis_size("depth")
    depth_rank = lax.axis_index("depth")
    total_depth = slab_count * depth_size
    block = min(128, extent)
    strip_width = extent // depth_size
    widened_rows = band_rows + 2 * MARGIN
    palette = make_palette(tf_table, total_depth)
    classified = classify(volume, palette)
    widened = extended(classified, (("band", 2),), MARGIN)
    finals = []
    for view_index in range(VIEWS):
        params = view_code[view_index]
        facing = params[3] >= 0
        picture = jnp.zeros((extent, 4, band_rows), jnp.float32)
        for step_index in range(slab_count):
            local_slice = jnp.where(facing, step_index, slab_count - 1 - step_index).astype(
                jnp.int32
            )
            global_slice = depth_rank * slab_count + local_slice
            whole_y, frac_y = split_offset(params[1], global_slice, total_depth)
            whole_x, frac_x = split_offset(params[0], global_slice, total_depth)
            current = lax.dynamic_index_in_dim(widened, local_slice, 1, keepdims=False)
            row_sheared = shear_columns(current, column_weights(whole_x, frac_x, block), block)
            sheared = shear_rows(
                row_sheared, row_weights(whole_y, frac_y, band_rows, widened_rows, MARGIN)
            )
            picture = over(picture, sheared)
        pieces = picture.reshape(depth_size, strip_width, 4, band_rows)
        arrived = lax.all_to_all(
            pieces.astype(jnp.bfloat16), "depth", split_axis=0, concat_axis=0, tiled=True
        ).astype(pieces.dtype)
        for level_index in range(depth_size.bit_length() - 1):
            paired = arrived.reshape((arrived.shape[0] // 2, 2) + arrived.shape[1:])
            earlier = paired[:, 0]
            later = paired[:, 1]
            front_part = jnp.where(facing, earlier, later)
            back_part = jnp.where(facing, later, earlier)
            arrived = over(front_part, back_part)
        strip = arrived[0]
        padded_strip = extended(strip, (("depth", 0),), MARGIN)
        weights = warp_weights(params[2], depth_rank * strip_width, strip_width, MARGIN, extent)
        final_strip = jnp.einsum(
            "ck,kay->cay",
            weights,
            padded_strip,
            precision=lax.Precision.HIGHEST,
            preferred_element_type=jnp.float32,
        )
        finals.append(final_strip)
    return jnp.stack(finals)


def solution(mesh):
    placed = (P("depth", "band", None), P(), P())
    return jax.shard_map(
        body, mesh=mesh, in_specs=placed, out_specs=P(None, "depth", None, "band"), check_vma=False
    )
```

profile of v0, /device:TPU:8, one launch (start us, length us, event | category | flops | bytes accessed | tf_op | source)
XLA Modules:
  0.0 122.0 jit_solution(5489275752223972056)
XLA Ops:
  0.9 24.4 %while.14 = (s32[]{:T(128)}, bf16[16,4,8,1024]{3,2,0,1:T(8,128)(2,1)S(1)}, s32[16,8,1024]{2,1,0:T(8,128)}, bf16[4,16,16]{2,1,0:T(8,128)(2,1)S(1)}, s32[]{:T(128)}) while((s32[]{:T(128)}, bf16[16,4,8,1024]{3,2,0,1:T(8,128)(2,1)S(1)}, s32[16,8,1024]{2,1,0:T(8,128)}, bf16[4,16,16]{2,1,0:T(8,128)(2,1)S(1)}, s32[]{:T(128)}) %tuple.78), condition=%wide.region_2.5_spmd.clone.clone, body=%wide.region_0.4_spmd.clone.clone.sunk | while | flops 18325504 | bytes 1411149 | solution.py:62
  25.5 1.3 %collective-permute-start.1 = (bf16[4,4,16,1024]{3,2,1,0:T(8,128)(2,1)S(1)}, bf16[4,4,16,1024]{3,2,1,0:T(8,128)(2,1)S(1)}, u32[]{:S(2)}, u32[]{:S(2)}) collective-permute-start(bf16[4,4,16,1024]{3,2,1,0:T(8,128)(2,1)S(1)} %get-tuple-element.149), channel_id=1, source_target_pairs={{1,0},{3,2},{5,4},{7,6},{9,8},{11,10},{13,12},{15,14},{17,16},{19,... | collective-permute-start | bytes 1572872 | tf_op jit(solution)/shard_map/ppermute | solution.py:19
  26.8 4.6 %collective-permute-start = (bf16[4,4,16,1024]{3,2,1,0:T(8,128)(2,1)S(1)}, bf16[4,4,16,1024]{3,2,1,0:T(8,128)(2,1)S(1)}, u32[]{:S(2)}, u32[]{:S(2)}) collective-permute-start(bf16[4,4,16,1024]{3,2,1,0:T(8,128)(2,1)S(1)} %get-tuple-element.148), channel_id=1, source_target_pairs={{0,1},{2,3},{4,5},{6,7},{8,9},{10,11},{12,13},{14,15},{16,17},{18,... | collective-permute-start | bytes 1572872 | tf_op jit(solution)/shard_map/ppermute | solution.py:18
  43.9 1.2 and_select_fusion
  45.1 1.2 convert_multiply_fusion
  48.5 1.7 %dynamic-slice_bitcast_fusion.4 = (bf16[4,64,1024]{2,1,0:T(8,128)(2,1)S(1)}, bf16[4,64,1024]{2,1,0:T(8,128)(2,1)}, bf16[4,64,1024]{2,1,0:T(8,128)(2,1)}, bf16[4,...) fusion(bf16[4,4,64,1024]{3,2,1,0:T(8,128)(2,1)S(1)} %pad_maximu, ...), kind=kLoop, calls=%fused_computation.126 | loop fusion | bytes 8388640 | tf_op jit(solution)/shard_map/jit(dynamic_index_in_dim)/squeeze | solution.py:138
  56.5 1.1 fusion.95
  61.5 1.1 fusion.98
  65.7 1.1 fusion.101
  67.0 1.1 fusion.104
  68.9 1.1 reshape.474
  70.0 6.3 %all-to-all-start.1 = ((bf16[16,2,4096]{2,1,0:T(2,128)(2,1)}), bf16[16,2,4096]{2,1,0:T(2,128)(2,1)S(1)}, u32[]{:S(2)}, u32[]{:S(2)}) async-start(bf16[16,2,4096]{2,1,0:T(2,128)(2,1)} %reshape.474), calls=%async_computation.1 | async-start | bytes 524288 | tf_op jit(solution)/shard_map/all_to_all | solution.py:145
  82.6 1.1 fusion.83
  87.3 1.1 fusion.86
  91.3 1.1 fusion.89
  92.4 1.1 fusion.92
  94.5 1.1 reshape.476
  95.6 6.0 %all-to-all-start = ((bf16[16,2,4096]{2,1,0:T(2,128)(2,1)}), bf16[16,2,4096]{2,1,0:T(2,128)(2,1)S(1)}, u32[]{:S(2)}, u32[]{:S(2)}) async-start(bf16[16,2,4096]{2,1,0:T(2,128)(2,1)} %reshape.476), calls=%async_computation | async-start | bytes 524288 | tf_op jit(solution)/shard_map/all_to_all | solution.py:145
  102.7 3.1 %collective-permute-start.5 = (f32[16,4,32]{0,2,1:T(8,128)S(1)}, f32[16,4,32]{0,2,1:T(8,128)S(1)}, u32[]{:S(2)}, u32[]{:S(2)}) collective-permute-start(f32[16,4,32]{0,2,1:T(8,128)S(1)} %get-tuple-element.157), channel_id=1, source_target_pairs={{2,0},{4,2},{6,4},{8,6},{10,8},{12,10},{14,12},{16,14},{18,16},{20... | collective-permute-start | bytes 24584 | tf_op jit(solution)/shard_map/ppermute | solution.py:19
  105.8 1.9 %collective-permute-start.4 = (f32[16,4,32]{0,2,1:T(8,128)S(1)}, f32[16,4,32]{0,2,1:T(8,128)S(1)}, u32[]{:S(2)}, u32[]{:S(2)}) collective-permute-start(f32[16,4,32]{0,2,1:T(8,128)S(1)} %get-tuple-element.156), channel_id=1, source_target_pairs={{0,2},{2,4},{4,6},{6,8},{8,10},{10,12},{12,14},{14,16},{16,18},{18... | collective-permute-start | bytes 24584 | tf_op jit(solution)/shard_map/ppermute | solution.py:18
  107.7 1.5 %all-to-all-done = bf16[16,2,4096]{2,1,0:T(2,128)(2,1)S(1)} async-done(((bf16[16,2,4096]{2,1,0:T(2,128)(2,1)}), bf16[16,2,4096]{2,1,0:T(2,128)(2,1)S(1)}, u32[]{:S(2)}, u32[]{:S(2)}) %all-to-all-start) | async-done | bytes 262176 | tf_op jit(solution)/shard_map/all_to_all | solution.py:145
  110.3 4.0 %collective-permute-start.3 = (f32[16,4,32]{0,2,1:T(8,128)S(1)}, f32[16,4,32]{0,2,1:T(8,128)S(1)}, u32[]{:S(2)}, u32[]{:S(2)}) collective-permute-start(f32[16,4,32]{0,2,1:T(8,128)S(1)} %get-tuple-element.155), channel_id=1, source_target_pairs={{2,0},{4,2},{6,4},{8,6},{10,8},{12,10},{14,12},{16,14},{18,16},{20... | collective-permute-start | bytes 24584 | tf_op jit(solution)/shard_map/ppermute | solution.py:19
  114.3 1.9 %collective-permute-start.2 = (f32[16,4,32]{0,2,1:T(8,128)S(1)}, f32[16,4,32]{0,2,1:T(8,128)S(1)}, u32[]{:S(2)}, u32[]{:S(2)}) collective-permute-start(f32[16,4,32]{0,2,1:T(8,128)S(1)} %get-tuple-element.154), channel_id=1, source_target_pairs={{0,2},{2,4},{4,6},{6,8},{8,10},{10,12},{12,14},{14,16},{16,18},{18... | collective-permute-start | bytes 24584 | tf_op jit(solution)/shard_map/ppermute | solution.py:18
  116.8 4.0 %collective-permute-done.2 = f32[16,4,32]{0,2,1:T(8,128)S(1)} collective-permute-done((f32[16,4,32]{0,2,1:T(8,128)S(1)}, f32[16,4,32]{0,2,1:T(8,128)S(1)}, u32[]{:S(2)}, u32[]{:S(2)}) %collective-permute-start.2) | collective-permute-done | bytes 8224 | tf_op jit(solution)/shard_map/ppermute | solution.py:18
  (241 shorter events, 59.1 us)
Async XLA Ops:
  25.3 6.0 %copy-start.22 = (s32[2,4]{1,0:T(2,128)S(1)}, s32[2,4]{1,0:T(2,128)}, u32[]{:S(2)}) copy-start(s32[2,4]{1,0:T(2,128)} %param.10) | copy-start | bytes 100
  25.5 22.7 %collective-permute-start.1 = (bf16[4,4,16,1024]{3,2,1,0:T(8,128)(2,1)S(1)}, bf16[4,4,16,1024]{3,2,1,0:T(8,128)(2,1)S(1)}, u32[]{:S(2)}, u32[]{:S(2)}) collective-permute-start(bf16[4,4,16,1024]{3,2,1,0:T(8,128)(2,1)S(1)} %get-tuple-element.149), channel_id=1, source_target_pairs={{1,0},{3,2},{5,4},{7,6},{9,8},{11,10},{13,12},{15,14},{17,16},{19,... | collective-permute-start | bytes 1572872 | tf_op jit(solution)/shard_map/ppermute | solution.py:19
  26.8 21.4 %collective-permute-start = (bf16[4,4,16,1024]{3,2,1,0:T(8,128)(2,1)S(1)}, bf16[4,4,16,1024]{3,2,1,0:T(8,128)(2,1)S(1)}, u32[]{:S(2)}, u32[]{:S(2)}) collective-permute-start(bf16[4,4,16,1024]{3,2,1,0:T(8,128)(2,1)S(1)} %get-tuple-element.148), channel_id=1, source_target_pairs={{0,1},{2,3},{4,5},{6,7},{8,9},{10,11},{12,13},{14,15},{16,17},{18,... | collective-permute-start | bytes 1572872 | tf_op jit(solution)/shard_map/ppermute | solution.py:18
  53.7 2.8 %copy-start.16 = (bf16[4,64,8,128]{3,1,2,0:T(8,128)(2,1)S(1)}, bf16[4,64,8,128]{3,1,2,0:T(8,128)(2,1)}, u32[]{:S(2)}) copy-start(bf16[4,64,8,128]{3,1,2,0:T(8,128)(2,1)} %copy.254) | copy-start | bytes 1572868
  53.7 2.8 %copy-start.18 = (bf16[4,64,8,128]{3,1,2,0:T(8,128)(2,1)S(1)}, bf16[4,64,8,128]{3,1,2,0:T(8,128)(2,1)}, u32[]{:S(2)}) copy-start(bf16[4,64,8,128]{3,1,2,0:T(8,128)(2,1)} %copy.253) | copy-start | bytes 1572868
  58.6 2.8 %copy-start.9 = (bf16[4,64,8,128]{3,1,2,0:T(8,128)(2,1)S(1)}, bf16[4,64,8,128]{3,1,2,0:T(8,128)(2,1)}, u32[]{:S(2)}) copy-start(bf16[4,64,8,128]{3,1,2,0:T(8,128)(2,1)} %copy.258) | copy-start | bytes 1572868
  58.6 2.8 %copy-start.11 = (bf16[4,64,8,128]{3,1,2,0:T(8,128)(2,1)S(1)}, bf16[4,64,8,128]{3,1,2,0:T(8,128)(2,1)}, u32[]{:S(2)}) copy-start(bf16[4,64,8,128]{3,1,2,0:T(8,128)(2,1)} %copy.257) | copy-start | bytes 1572868
  58.6 2.8 %copy-start.14 = (bf16[4,64,8,128]{3,1,2,0:T(8,128)(2,1)S(1)}, bf16[4,64,8,128]{3,1,2,0:T(8,128)(2,1)}, u32[]{:S(2)}) copy-start(bf16[4,64,8,128]{3,1,2,0:T(8,128)(2,1)} %copy.256) | copy-start | bytes 1572868
  68.1 8.1 %copy-start.2 = (bf16[4,64,1024]{2,1,0:T(8,128)(2,1)S(1)}, bf16[4,64,1024]{2,1,0:T(8,128)(2,1)}, u32[]{:S(2)}) copy-start(bf16[4,64,1024]{2,1,0:T(8,128)(2,1)} %get-tuple-element.119) | copy-start | bytes 1572868
  70.0 25.6 %all-to-all-start.1 = ((bf16[16,2,4096]{2,1,0:T(2,128)(2,1)}), bf16[16,2,4096]{2,1,0:T(2,128)(2,1)S(1)}, u32[]{:S(2)}, u32[]{:S(2)}) async-start(bf16[16,2,4096]{2,1,0:T(2,128)(2,1)} %reshape.474), calls=%async_computation.1 | async-start | bytes 524288 | tf_op jit(solution)/shard_map/all_to_all | solution.py:145
  79.7 2.8 %copy-start.17 = (bf16[4,64,8,128]{3,1,2,0:T(8,128)(2,1)S(1)}, bf16[4,64,8,128]{3,1,2,0:T(8,128)(2,1)}, u32[]{:S(2)}) copy-start(bf16[4,64,8,128]{3,1,2,0:T(8,128)(2,1)} %copy.242) | copy-start | bytes 1572868
  79.7 2.8 %copy-start.19 = (bf16[4,64,8,128]{3,1,2,0:T(8,128)(2,1)S(1)}, bf16[4,64,8,128]{3,1,2,0:T(8,128)(2,1)}, u32[]{:S(2)}) copy-start(bf16[4,64,8,128]{3,1,2,0:T(8,128)(2,1)} %copy.241) | copy-start | bytes 1572868
  82.6 2.0 %copy-start = (bf16[4,64,1024]{2,1,0:T(8,128)(2,1)S(1)}, bf16[4,64,1024]{2,1,0:T(8,128)(2,1)}, u32[]{:S(2)}) copy-start(bf16[4,64,1024]{2,1,0:T(8,128)(2,1)} %get-tuple-element.117) | copy-start | bytes 1572868
  85.3 2.0 %copy-start.10 = (bf16[4,64,8,128]{3,1,2,0:T(8,128)(2,1)S(1)}, bf16[4,64,8,128]{3,1,2,0:T(8,128)(2,1)}, u32[]{:S(2)}) copy-start(bf16[4,64,8,128]{3,1,2,0:T(8,128)(2,1)} %copy.246) | copy-start | bytes 1572868
  85.3 2.0 %copy-start.13 = (bf16[4,64,8,128]{3,1,2,0:T(8,128)(2,1)S(1)}, bf16[4,64,8,128]{3,1,2,0:T(8,128)(2,1)}, u32[]{:S(2)}) copy-start(bf16[4,64,8,128]{3,1,2,0:T(8,128)(2,1)} %copy.245) | copy-start | bytes 1572868
  85.3 2.0 %copy-start.15 = (bf16[4,64,8,128]{3,1,2,0:T(8,128)(2,1)S(1)}, bf16[4,64,8,128]{3,1,2,0:T(8,128)(2,1)}, u32[]{:S(2)}) copy-start(bf16[4,64,8,128]{3,1,2,0:T(8,128)(2,1)} %copy.244) | copy-start | bytes 1572868
  95.6 13.6 %all-to-all-start = ((bf16[16,2,4096]{2,1,0:T(2,128)(2,1)}), bf16[16,2,4096]{2,1,0:T(2,128)(2,1)S(1)}, u32[]{:S(2)}, u32[]{:S(2)}) async-start(bf16[16,2,4096]{2,1,0:T(2,128)(2,1)} %reshape.476), calls=%async_computation | async-start | bytes 524288 | tf_op jit(solution)/shard_map/all_to_all | solution.py:145
  102.7 13.6 %collective-permute-start.5 = (f32[16,4,32]{0,2,1:T(8,128)S(1)}, f32[16,4,32]{0,2,1:T(8,128)S(1)}, u32[]{:S(2)}, u32[]{:S(2)}) collective-permute-start(f32[16,4,32]{0,2,1:T(8,128)S(1)} %get-tuple-element.157), channel_id=1, source_target_pairs={{2,0},{4,2},{6,4},{8,6},{10,8},{12,10},{14,12},{16,14},{18,16},{20... | collective-permute-start | bytes 24584 | tf_op jit(solution)/shard_map/ppermute | solution.py:19
  105.8 10.5 %collective-permute-start.4 = (f32[16,4,32]{0,2,1:T(8,128)S(1)}, f32[16,4,32]{0,2,1:T(8,128)S(1)}, u32[]{:S(2)}, u32[]{:S(2)}) collective-permute-start(f32[16,4,32]{0,2,1:T(8,128)S(1)} %get-tuple-element.156), channel_id=1, source_target_pairs={{0,2},{2,4},{4,6},{6,8},{8,10},{10,12},{12,14},{14,16},{16,18},{18... | collective-permute-start | bytes 24584 | tf_op jit(solution)/shard_map/ppermute | solution.py:18
  109.9 6.5 %copy-start.23 = (s32[64]{0:T(128)S(1)}, s32[64]{0:T(128)}, u32[]{:S(2)}) copy-start(s32[64]{0:T(128)} %and_select_fusion) | copy-start | bytes 772
  109.9 6.5 %copy-start.24 = (f32[64]{0:T(128)S(1)}, f32[64]{0:T(128)}, u32[]{:S(2)}) copy-start(f32[64]{0:T(128)} %convert_multiply_fusion) | copy-start | bytes 772
  109.9 6.5 %copy-start.25 = (s32[96]{0:T(128)S(1)}, s32[96]{0:T(128)}, u32[]{:S(2)}) copy-start(s32[96]{0:T(128)} %iota_add_fusion.2) | copy-start | bytes 1156
  110.3 6.5 %collective-permute-start.3 = (f32[16,4,32]{0,2,1:T(8,128)S(1)}, f32[16,4,32]{0,2,1:T(8,128)S(1)}, u32[]{:S(2)}, u32[]{:S(2)}) collective-permute-start(f32[16,4,32]{0,2,1:T(8,128)S(1)} %get-tuple-element.155), channel_id=1, source_target_pairs={{2,0},{4,2},{6,4},{8,6},{10,8},{12,10},{14,12},{16,14},{18,16},{20... | collective-permute-start | bytes 24584 | tf_op jit(solution)/shard_map/ppermute | solution.py:19
  114.3 6.5 %collective-permute-start.2 = (f32[16,4,32]{0,2,1:T(8,128)S(1)}, f32[16,4,32]{0,2,1:T(8,128)S(1)}, u32[]{:S(2)}, u32[]{:S(2)}) collective-permute-start(f32[16,4,32]{0,2,1:T(8,128)S(1)} %get-tuple-element.154), channel_id=1, source_target_pairs={{0,2},{2,4},{4,6},{6,8},{8,10},{10,12},{12,14},{14,16},{16,18},{18... | collective-permute-start | bytes 24584 | tf_op jit(solution)/shard_map/ppermute | solution.py:18
  (10 other events, 12.3 us)
where the time goes:
time: 124 us; the launch traced here: 122 us
  local copies, waits for them, and re-layouts  30.6 us (25%)
  starting transfers between devices  29.1 us (23%)
  other arithmetic  22 us (18%)
  matrix products  21.2 us (17%)
  between operations  12.9 us (10%)
  waiting for transfers between devices  5.49 us (4%)
    unnamed x80, local copies, waits for them, and re-layouts  20.5 us
    eq x16, other arithmetic, lookup(): low_hot = (low_part[None] == levels[:, None, None]).astype(jnp.bfloat16)  12.6 us
    all_to_all x2, starting transfers between devices, body(): lax.all_to_all(pieces.astype(jnp.bfloat16), 'depth', split_axis=0, concat...  12.3 us
    dot_general x16, matrix products, lookup(): jnp.einsum('chl,lgk->chgk', table, low_hot, preferred_element_type=jnp.fl...  10.1 us
    dot_general x8, matrix products, shear_columns(): jnp.einsum('crbk,kj->bjcr', windows, tap_matrix, preferred_element_type=j...  8.45 us
    ppermute x3, starting transfers between devices, extended(): before = lax.ppermute(last, axis, up)  8.45 us
    ppermute x3, starting transfers between devices, extended(): after = lax.ppermute(first, axis, down)  8.41 us
    ppermute x3, waiting for transfers between devices, extended(): before = lax.ppermute(last, axis, up)  4.03 us
  transfers between devices with their start and end apart: 8, of which 2 were waited for; matrix products, arithmetic and copies ran while one was open for 21% of the time, Pallas kernels for 0%

commit v1 on v0

--- a/solution.py
+++ b/solution.py
@@ -1,3 +1,4 @@
+import functools
 import math
 import jax
 import jax.numpy as jnp
@@ -6,6 +7,42 @@
 
 VIEWS = 2
 MARGIN = 16
+
+
+def advance_shelves_for(vec, on_dim, mine):
+    work_now = vec.shape
+    piece_next = vec.reshape(
+        *work_now[:on_dim], mine, work_now[on_dim] // mine, *work_now[on_dim + 1 :]
+    )
+    return jnp.moveaxis(piece_next, on_dim, 0)
+
+
+def see_pairs_all_on(vector, join_dim):
+    mid_arr = list(vector.shape[1:])
+    mid_arr[join_dim] *= vector.shape[0]
+    return jnp.moveaxis(vector, 0, join_dim).reshape(mid_arr)
+
+
+def time_rings_over_axis(u, named_axis, work_x, s0):
+    y = lax.axis_index(named_axis)
+    p_next = lax.axis_size(named_axis)
+    b_next, arr_now = (p_next, y)
+    current_block = advance_shelves_for(u, work_x, b_next)
+    dev = 1
+    blocks_here = [current_block[arr_now]]
+    while dev < b_next:
+        found_now = current_block[(arr_now + dev) % b_next]
+        new = lax.ppermute(
+            found_now, named_axis, perm=[(c, (c + dev) % b_next) for c in range(b_next)]
+        )
+        blocks_here.append(new)
+        dev = dev + 1
+    z = jnp.stack(blocks_here)
+    current_block = z[(arr_now - jnp.arange(b_next)) % b_next]
+    return see_pairs_all_on(current_block, s0)
+
+
+_meet_trails = functools.partial(time_rings_over_axis, named_axis="depth", work_x=0, s0=0)
 
 
 def extended(x, sides, width):
@@ -142,9 +179,7 @@
             )
             picture = over(picture, sheared)
         pieces = picture.reshape(depth_size, strip_width, 4, band_rows)
-        arrived = lax.all_to_all(
-            pieces.astype(jnp.bfloat16), "depth", split_axis=0, concat_axis=0, tiled=True
-        ).astype(pieces.dtype)
+        arrived = _meet_trails(pieces.astype(jnp.bfloat16)).astype(pieces.dtype)
         for level_index in range(depth_size.bit_length() - 1):
             paired = arrived.reshape((arrived.shape[0] // 2, 2) + arrived.shape[1:])
             earlier = paired[:, 0]

time: 124 us -> 155 us (1.25)
  starting transfers between devices: 29.1 us -> 60.4 us
  local copies, waits for them, and re-layouts: 30.6 us -> 34.1 us
  other arithmetic: 22 us -> 19 us
    ppermute x0 -> x30, starting transfers between devices: none -> 44.2 us  [time_rings_over_axis(): lax.ppermute(found_now, named_axis, perm=[(c, (c + dev) % b_next) for c i...]
    all_to_all x2 -> x0, starting transfers between devices: 12.3 us -> none  [body(): lax.all_to_all(pieces.astype(jnp.bfloat16), 'depth', split_axis=0, concat...]
    squeeze x0 -> x1, local copies, waits for them, and re-layouts: none -> 3.75 us  [time_rings_over_axis(): found_now = current_block[(arr_now + dev) % b_next]]
    unnamed x80 -> x126, local copies, waits for them, and re-layouts: 20.5 us -> 19 us
  transfers between devices with their start and end apart: 8 -> 36, of which waited for: 2 -> 1; matrix products, arithmetic and copies ran while one was open for 21% -> 4% of each run, Pallas kernels for 0% -> 0%
where the time goes in v1:
time: 155 us; the launch traced here: 153 us
  starting transfers between devices  60.4 us (39%)
  local copies, waits for them, and re-layouts  34.1 us (22%)
  matrix products  21.2 us (14%)
  other arithmetic  19 us (12%)
  between operations  13.6 us (9%)
  waiting for transfers between devices  4.14 us (3%)
    ppermute x30, starting transfers between devices, time_rings_over_axis(): lax.ppermute(found_now, named_axis, perm=[(c, (c + dev) % b_next) for c i...  44.2 us
    unnamed x126, local copies, waits for them, and re-layouts  19 us
    eq x16, other arithmetic, lookup(): low_hot = (low_part[None] == levels[:, None, None]).astype(jnp.bfloat16)  12.6 us
    dot_general x16, matrix products, lookup(): jnp.einsum('chl,lgk->chgk', table, low_hot, preferred_element_type=jnp.fl...  10.1 us
    ppermute x3, starting transfers between devices, extended(): before = lax.ppermute(last, axis, up)  8.92 us
    dot_general x8, matrix products, shear_columns(): jnp.einsum('crbk,kj->bjcr', windows, tap_matrix, preferred_element_type=j...  8.45 us
    ppermute x3, starting transfers between devices, extended(): after = lax.ppermute(first, axis, down)  7.3 us
    ppermute x3, waiting for transfers between devices, extended(): before = lax.ppermute(last, axis, up)  4.06 us
  transfers between devices with their start and end apart: 36, of which 1 were waited for; matrix products, arithmetic and copies ran while one was open for 4% of the time, Pallas kernels for 0%

profile of v1, /device:TPU:8, one launch (start us, length us, event | category | flops | bytes accessed | tf_op | source)
XLA Modules:
  0.0 153.2 jit_solution(16823028119471408063)
XLA Ops:
  0.9 24.4 %while.14 = (s32[]{:T(128)}, bf16[16,4,8,1024]{3,2,0,1:T(8,128)(2,1)S(1)}, s32[16,8,1024]{2,1,0:T(8,128)}, bf16[4,16,16]{2,1,0:T(8,128)(2,1)S(1)}, s32[]{:T(128)}) while((s32[]{:T(128)}, bf16[16,4,8,1024]{3,2,0,1:T(8,128)(2,1)S(1)}, s32[16,8,1024]{2,1,0:T(8,128)}, bf16[4,16,16]{2,1,0:T(8,128)(2,1)S(1)}, ...), condition=%wide.region_2.5_spmd.clone.clone, body=%wide.region_0.4_spmd.clone.clone.sunk | while | flops 18325504 | bytes 1411149 | solution.py:99
  26.8 4.6 %collective-permute-start = (bf16[4,4,16,1024]{3,2,1,0:T(8,128)(2,1)S(1)}, bf16[4,4,16,1024]{3,2,1,0:T(8,128)(2,1)S(1)}, u32[]{:S(2)}, u32[]{:S(2)}) collective-permute-start(bf16[4,4,16,1024]{3,2,1,0:T(8,128)(2,1)S(1)} %get-tuple-element.148), channel_id=1, source_target_pairs={{0,1},{2,3},{4,5},{6,7},{8,9},{10,11},{12,13},{14,15},{16,17},{18,... | collective-permute-start | bytes 1572872 | tf_op jit(solution)/shard_map/ppermute | solution.py:55
  47.1 1.7 %dynamic-slice_bitcast_fusion.4 = (bf16[4,64,1024]{2,1,0:T(8,128)(2,1)}, bf16[4,64,1024]{2,1,0:T(8,128)(2,1)}, bf16[4,64,1024]{2,1,0:T(8,128)(2,1)}, bf16[4,64,1...) fusion(bf16[4,4,64,1024]{3,2,1,0:T(8,128)(2,1)S(1)} %pad_maximu, ...), kind=kLoop, calls=%fused_computation.127 | loop fusion | bytes 8388640 | tf_op jit(solution)/shard_map/jit(dynamic_index_in_dim)/squeeze | solution.py:175
  85.3 3.7 %constant_dynamic-slice_fusion = (bf16[1,64,4,32]{1,0,3,2:T(2,128)(2,1)S(1)}, bf16[1,64,4,32]{1,0,3,2:T(2,128)(2,1)S(1)}, bf16[1,64,4,32]{1,0,3,2:T(2,128)(2,1)S...) fusion(bf16[16,64,4,32]{1,0,3,2:T(8,128)(2,1)S(1)} %convert_ele, ...), kind=kLoop, calls=%fused_computation.1374 | loop fusion | bytes 1048640 | tf_op jit(solution)/shard_map/squeeze | solution.py:34
  90.7 2.5 %collective-permute-start.21 = (bf16[1,64,4,32]{1,3,2,0:T(8,128)(2,1)S(1)}, bf16[1,64,4,32]{1,3,2,0:T(8,128)(2,1)S(1)}, u32[]{:S(2)}, u32[]{:S(2)}) collective-permute-start(bf16[1,64,4,32]{1,3,2,0:T(8,128)(2,1)S(1)} %copy.319), channel_id=1, source_target_pairs={{0,6},{2,8},{4,10},{6,12},{8,14},{10,16},{12,18},{14,20},{16,22},{... | collective-permute-start | bytes 49160 | tf_op jit(solution)/shard_map/ppermute | solution.py:35
  93.2 1.6 %collective-permute-start.22 = (bf16[1,64,4,32]{1,3,2,0:T(8,128)(2,1)S(1)}, bf16[1,64,4,32]{1,3,2,0:T(8,128)(2,1)S(1)}, u32[]{:S(2)}, u32[]{:S(2)}) collective-permute-start(bf16[1,64,4,32]{1,3,2,0:T(8,128)(2,1)S(1)} %copy.320), channel_id=1, source_target_pairs={{0,8},{2,10},{4,12},{6,14},{8,16},{10,18},{12,20},{14,22},{16,24},... | collective-permute-start | bytes 49160 | tf_op jit(solution)/shard_map/ppermute | solution.py:35
  96.9 2.3 %collective-permute-start.25 = (bf16[1,64,4,32]{1,3,2,0:T(8,128)(2,1)S(1)}, bf16[1,64,4,32]{1,3,2,0:T(8,128)(2,1)S(1)}, u32[]{:S(2)}, u32[]{:S(2)}) collective-permute-start(bf16[1,64,4,32]{1,3,2,0:T(8,128)(2,1)S(1)} %copy.323), channel_id=1, source_target_pairs={{0,14},{2,16},{4,18},{6,20},{8,22},{10,24},{12,26},{14,28},{16,30}... | collective-permute-start | bytes 49160 | tf_op jit(solution)/shard_map/ppermute | solution.py:35
  99.2 3.4 %collective-permute-start.26 = (bf16[1,64,4,32]{1,3,2,0:T(8,128)(2,1)S(1)}, bf16[1,64,4,32]{1,3,2,0:T(8,128)(2,1)S(1)}, u32[]{:S(2)}, u32[]{:S(2)}) collective-permute-start(bf16[1,64,4,32]{1,3,2,0:T(8,128)(2,1)S(1)} %copy.324), channel_id=1, source_target_pairs={{0,16},{2,18},{4,20},{6,22},{8,24},{10,26},{12,28},{14,30},{16,0},... | collective-permute-start | bytes 49160 | tf_op jit(solution)/shard_map/ppermute | solution.py:35
  104.1 2.5 %collective-permute-start.29 = (bf16[1,64,4,32]{1,3,2,0:T(8,128)(2,1)S(1)}, bf16[1,64,4,32]{1,3,2,0:T(8,128)(2,1)S(1)}, u32[]{:S(2)}, u32[]{:S(2)}) collective-permute-start(bf16[1,64,4,32]{1,3,2,0:T(8,128)(2,1)S(1)} %copy.327), channel_id=1, source_target_pairs={{0,22},{2,24},{4,26},{6,28},{8,30},{10,0},{12,2},{14,4},{16,6},{18... | collective-permute-start | bytes 49160 | tf_op jit(solution)/shard_map/ppermute | solution.py:35
  108.1 2.1 %collective-permute-start.32 = (bf16[1,64,4,32]{1,3,2,0:T(8,128)(2,1)S(1)}, bf16[1,64,4,32]{1,3,2,0:T(8,128)(2,1)S(1)}, u32[]{:S(2)}, u32[]{:S(2)}) collective-permute-start(bf16[1,64,4,32]{1,3,2,0:T(8,128)(2,1)S(1)} %copy.330), channel_id=1, source_target_pairs={{0,28},{2,30},{4,0},{6,2},{8,4},{10,6},{12,8},{14,10},{16,12},{18,... | collective-permute-start | bytes 49160 | tf_op jit(solution)/shard_map/ppermute | solution.py:35
  110.2 2.1 %collective-permute-start.33 = (bf16[1,64,4,32]{1,3,2,0:T(8,128)(2,1)S(1)}, bf16[1,64,4,32]{1,3,2,0:T(8,128)(2,1)S(1)}, u32[]{:S(2)}, u32[]{:S(2)}) collective-permute-start(bf16[1,64,4,32]{1,3,2,0:T(8,128)(2,1)S(1)} %copy.331), channel_id=1, source_target_pairs={{0,30},{2,0},{4,2},{6,4},{8,6},{10,8},{12,10},{14,12},{16,14},{18,... | collective-permute-start | bytes 49160 | tf_op jit(solution)/shard_map/ppermute | solution.py:35
  115.0 2.6 %collective-permute-start.6 = (bf16[1,64,4,32]{1,3,2,0:T(8,128)(2,1)S(1)}, bf16[1,64,4,32]{1,3,2,0:T(8,128)(2,1)S(1)}, u32[]{:S(2)}, u32[]{:S(2)}) collective-permute-start(bf16[1,64,4,32]{1,3,2,0:T(8,128)(2,1)S(1)} %copy.291), channel_id=1, source_target_pairs={{0,10},{2,12},{4,14},{6,16},{8,18},{10,20},{12,22},{14,24},{16,26}... | collective-permute-start | bytes 49160 | tf_op jit(solution)/shard_map/ppermute | solution.py:35
  119.0 1.9 %collective-permute-start.7 = (bf16[1,64,4,32]{1,3,2,0:T(8,128)(2,1)S(1)}, bf16[1,64,4,32]{1,3,2,0:T(8,128)(2,1)S(1)}, u32[]{:S(2)}, u32[]{:S(2)}) collective-permute-start(bf16[1,64,4,32]{1,3,2,0:T(8,128)(2,1)S(1)} %copy.292), channel_id=1, source_target_pairs={{0,12},{2,14},{4,16},{6,18},{8,20},{10,22},{12,24},{14,26},{16,28}... | collective-permute-start | bytes 49160 | tf_op jit(solution)/shard_map/ppermute | solution.py:35
  120.9 3.2 %collective-permute-start.8 = (bf16[1,64,4,32]{1,3,2,0:T(8,128)(2,1)S(1)}, bf16[1,64,4,32]{1,3,2,0:T(8,128)(2,1)S(1)}, u32[]{:S(2)}, u32[]{:S(2)}) collective-permute-start(bf16[1,64,4,32]{1,3,2,0:T(8,128)(2,1)S(1)} %copy.293), channel_id=1, source_target_pairs={{0,14},{2,16},{4,18},{6,20},{8,22},{10,24},{12,26},{14,28},{16,30}... | collective-permute-start | bytes 49160 | tf_op jit(solution)/shard_map/ppermute | solution.py:35
  124.1 1.9 %collective-permute-start.9 = (bf16[1,64,4,32]{1,3,2,0:T(8,128)(2,1)S(1)}, bf16[1,64,4,32]{1,3,2,0:T(8,128)(2,1)S(1)}, u32[]{:S(2)}, u32[]{:S(2)}) collective-permute-start(bf16[1,64,4,32]{1,3,2,0:T(8,128)(2,1)S(1)} %copy.294), channel_id=1, source_target_pairs={{0,16},{2,18},{4,20},{6,22},{8,24},{10,26},{12,28},{14,30},{16,0},... | collective-permute-start | bytes 49160 | tf_op jit(solution)/shard_map/ppermute | solution.py:35
  126.1 2.1 %collective-permute-start.11 = (bf16[1,64,4,32]{1,3,2,0:T(8,128)(2,1)S(1)}, bf16[1,64,4,32]{1,3,2,0:T(8,128)(2,1)S(1)}, u32[]{:S(2)}, u32[]{:S(2)}) collective-permute-start(bf16[1,64,4,32]{1,3,2,0:T(8,128)(2,1)S(1)} %copy.296), channel_id=1, source_target_pairs={{0,20},{2,22},{4,24},{6,26},{8,28},{10,30},{12,0},{14,2},{16,4},{1... | collective-permute-start | bytes 49160 | tf_op jit(solution)/shard_map/ppermute | solution.py:35
  128.2 1.6 %collective-permute-start.12 = (bf16[1,64,4,32]{1,3,2,0:T(8,128)(2,1)S(1)}, bf16[1,64,4,32]{1,3,2,0:T(8,128)(2,1)S(1)}, u32[]{:S(2)}, u32[]{:S(2)}) collective-permute-start(bf16[1,64,4,32]{1,3,2,0:T(8,128)(2,1)S(1)} %copy.297), channel_id=1, source_target_pairs={{0,22},{2,24},{4,26},{6,28},{8,30},{10,0},{12,2},{14,4},{16,6},{18... | collective-permute-start | bytes 49160 | tf_op jit(solution)/shard_map/ppermute | solution.py:35
  129.8 2.3 %collective-permute-start.13 = (bf16[1,64,4,32]{1,3,2,0:T(8,128)(2,1)S(1)}, bf16[1,64,4,32]{1,3,2,0:T(8,128)(2,1)S(1)}, u32[]{:S(2)}, u32[]{:S(2)}) collective-permute-start(bf16[1,64,4,32]{1,3,2,0:T(8,128)(2,1)S(1)} %copy.298), channel_id=1, source_target_pairs={{0,24},{2,26},{4,28},{6,30},{8,0},{10,2},{12,4},{14,6},{16,8},{18,... | collective-permute-start | bytes 49160 | tf_op jit(solution)/shard_map/ppermute | solution.py:35
  132.2 2.4 %collective-permute-start.15 = (bf16[1,64,4,32]{1,3,2,0:T(8,128)(2,1)S(1)}, bf16[1,64,4,32]{1,3,2,0:T(8,128)(2,1)S(1)}, u32[]{:S(2)}, u32[]{:S(2)}) collective-permute-start(bf16[1,64,4,32]{1,3,2,0:T(8,128)(2,1)S(1)} %copy.300), channel_id=1, source_target_pairs={{0,28},{2,30},{4,0},{6,2},{8,4},{10,6},{12,8},{14,10},{16,12},{18,... | collective-permute-start | bytes 49160 | tf_op jit(solution)/shard_map/ppermute | solution.py:35
  135.6 1.9 %collective-permute-start.35 = (f32[16,4,32]{0,2,1:T(8,128)S(1)}, f32[16,4,32]{0,2,1:T(8,128)S(1)}, u32[]{:S(2)}, u32[]{:S(2)}) collective-permute-start(f32[16,4,32]{0,2,1:T(8,128)S(1)} %get-tuple-element.189), channel_id=1, source_target_pairs={{2,0},{4,2},{6,4},{8,6},{10,8},{12,10},{14,12},{16,14},{18,16},{20... | collective-permute-start | bytes 24584 | tf_op jit(solution)/shard_map/ppermute | solution.py:56
  137.6 2.4 %collective-permute-start.34 = (f32[16,4,32]{0,2,1:T(8,128)S(1)}, f32[16,4,32]{0,2,1:T(8,128)S(1)}, u32[]{:S(2)}, u32[]{:S(2)}) collective-permute-start(f32[16,4,32]{0,2,1:T(8,128)S(1)} %get-tuple-element.188), channel_id=1, source_target_pairs={{0,2},{2,4},{4,6},{6,8},{8,10},{10,12},{12,14},{14,16},{16,18},{18... | collective-permute-start | bytes 24584 | tf_op jit(solution)/shard_map/ppermute | solution.py:55
  141.5 4.1 %collective-permute-start.18 = (f32[16,4,32]{0,2,1:T(8,128)S(1)}, f32[16,4,32]{0,2,1:T(8,128)S(1)}, u32[]{:S(2)}, u32[]{:S(2)}) collective-permute-start(f32[16,4,32]{0,2,1:T(8,128)S(1)} %get-tuple-element.187), channel_id=1, source_target_pairs={{2,0},{4,2},{6,4},{8,6},{10,8},{12,10},{14,12},{16,14},{18,16},{20... | collective-permute-start | bytes 24584 | tf_op jit(solution)/shard_map/ppermute | solution.py:56
  145.5 1.9 %collective-permute-start.17 = (f32[16,4,32]{0,2,1:T(8,128)S(1)}, f32[16,4,32]{0,2,1:T(8,128)S(1)}, u32[]{:S(2)}, u32[]{:S(2)}) collective-permute-start(f32[16,4,32]{0,2,1:T(8,128)S(1)} %get-tuple-element.186), channel_id=1, source_target_pairs={{0,2},{2,4},{4,6},{6,8},{8,10},{10,12},{12,14},{14,16},{16,18},{18... | collective-permute-start | bytes 24584 | tf_op jit(solution)/shard_map/ppermute | solution.py:55
  148.0 4.1 %collective-permute-done.17 = f32[16,4,32]{0,2,1:T(8,128)S(1)} collective-permute-done((f32[16,4,32]{0,2,1:T(8,128)S(1)}, f32[16,4,32]{0,2,1:T(8,128)S(1)}, u32[]{:S(2)}, u32[]{:S(2)}) %collective-permute-start.17) | collective-permute-done | bytes 8224 | tf_op jit(solution)/shard_map/ppermute | solution.py:55
  (348 shorter events, 80.0 us)
Async XLA Ops:
  25.5 21.4 %collective-permute-start.1 = (bf16[4,4,16,1024]{3,2,1,0:T(8,128)(2,1)S(1)}, bf16[4,4,16,1024]{3,2,1,0:T(8,128)(2,1)S(1)}, u32[]{:S(2)}, u32[]{:S(2)}) collective-permute-start(bf16[4,4,16,1024]{3,2,1,0:T(8,128)(2,1)S(1)} %get-tuple-element.149), channel_id=1, source_target_pairs={{1,0},{3,2},{5,4},{7,6},{9,8},{11,10},{13,12},{15,14},{17,16},{19,... | collective-permute-start | bytes 1572872 | tf_op jit(solution)/shard_map/ppermute | solution.py:56
  26.8 20.1 %collective-permute-start = (bf16[4,4,16,1024]{3,2,1,0:T(8,128)(2,1)S(1)}, bf16[4,4,16,1024]{3,2,1,0:T(8,128)(2,1)S(1)}, u32[]{:S(2)}, u32[]{:S(2)}) collective-permute-start(bf16[4,4,16,1024]{3,2,1,0:T(8,128)(2,1)S(1)} %get-tuple-element.148), channel_id=1, source_target_pairs={{0,1},{2,3},{4,5},{6,7},{8,9},{10,11},{12,13},{14,15},{16,17},{18,... | collective-permute-start | bytes 1572872 | tf_op jit(solution)/shard_map/ppermute | solution.py:55
  89.2 7.8 %collective-permute-start.20 = (bf16[1,64,4,32]{1,3,2,0:T(8,128)(2,1)S(1)}, bf16[1,64,4,32]{1,3,2,0:T(8,128)(2,1)S(1)}, u32[]{:S(2)}, u32[]{:S(2)}) collective-permute-start(bf16[1,64,4,32]{1,3,2,0:T(8,128)(2,1)S(1)} %copy.318), channel_id=1, source_target_pairs={{0,4},{2,6},{4,8},{6,10},{8,12},{10,14},{12,16},{14,18},{16,20},{1... | collective-permute-start | bytes 49160 | tf_op jit(solution)/shard_map/ppermute | solution.py:35
  90.7 8.5 %collective-permute-start.21 = (bf16[1,64,4,32]{1,3,2,0:T(8,128)(2,1)S(1)}, bf16[1,64,4,32]{1,3,2,0:T(8,128)(2,1)S(1)}, u32[]{:S(2)}, u32[]{:S(2)}) collective-permute-start(bf16[1,64,4,32]{1,3,2,0:T(8,128)(2,1)S(1)} %copy.319), channel_id=1, source_target_pairs={{0,6},{2,8},{4,10},{6,12},{8,14},{10,16},{12,18},{14,20},{16,22},{... | collective-permute-start | bytes 49160 | tf_op jit(solution)/shard_map/ppermute | solution.py:35
  93.2 9.5 %collective-permute-start.22 = (bf16[1,64,4,32]{1,3,2,0:T(8,128)(2,1)S(1)}, bf16[1,64,4,32]{1,3,2,0:T(8,128)(2,1)S(1)}, u32[]{:S(2)}, u32[]{:S(2)}) collective-permute-start(bf16[1,64,4,32]{1,3,2,0:T(8,128)(2,1)S(1)} %copy.320), channel_id=1, source_target_pairs={{0,8},{2,10},{4,12},{6,14},{8,16},{10,18},{12,20},{14,22},{16,24},... | collective-permute-start | bytes 49160 | tf_op jit(solution)/shard_map/ppermute | solution.py:35
  94.8 7.9 %collective-permute-start.23 = (bf16[1,64,4,32]{1,3,2,0:T(8,128)(2,1)S(1)}, bf16[1,64,4,32]{1,3,2,0:T(8,128)(2,1)S(1)}, u32[]{:S(2)}, u32[]{:S(2)}) collective-permute-start(bf16[1,64,4,32]{1,3,2,0:T(8,128)(2,1)S(1)} %copy.321), channel_id=1, source_target_pairs={{0,10},{2,12},{4,14},{6,16},{8,18},{10,20},{12,22},{14,24},{16,26}... | collective-permute-start | bytes 49160 | tf_op jit(solution)/shard_map/ppermute | solution.py:35
  95.5 8.6 %collective-permute-start.24 = (bf16[1,64,4,32]{1,3,2,0:T(8,128)(2,1)S(1)}, bf16[1,64,4,32]{1,3,2,0:T(8,128)(2,1)S(1)}, u32[]{:S(2)}, u32[]{:S(2)}) collective-permute-start(bf16[1,64,4,32]{1,3,2,0:T(8,128)(2,1)S(1)} %copy.322), channel_id=1, source_target_pairs={{0,12},{2,14},{4,16},{6,18},{8,20},{10,22},{12,24},{14,26},{16,28}... | collective-permute-start | bytes 49160 | tf_op jit(solution)/shard_map/ppermute | solution.py:35
  96.9 9.7 %collective-permute-start.25 = (bf16[1,64,4,32]{1,3,2,0:T(8,128)(2,1)S(1)}, bf16[1,64,4,32]{1,3,2,0:T(8,128)(2,1)S(1)}, u32[]{:S(2)}, u32[]{:S(2)}) collective-permute-start(bf16[1,64,4,32]{1,3,2,0:T(8,128)(2,1)S(1)} %copy.323), channel_id=1, source_target_pairs={{0,14},{2,16},{4,18},{6,20},{8,22},{10,24},{12,26},{14,28},{16,30}... | collective-permute-start | bytes 49160 | tf_op jit(solution)/shard_map/ppermute | solution.py:35
  99.2 8.8 %collective-permute-start.26 = (bf16[1,64,4,32]{1,3,2,0:T(8,128)(2,1)S(1)}, bf16[1,64,4,32]{1,3,2,0:T(8,128)(2,1)S(1)}, u32[]{:S(2)}, u32[]{:S(2)}) collective-permute-start(bf16[1,64,4,32]{1,3,2,0:T(8,128)(2,1)S(1)} %copy.324), channel_id=1, source_target_pairs={{0,16},{2,18},{4,20},{6,22},{8,24},{10,26},{12,28},{14,30},{16,0},... | collective-permute-start | bytes 49160 | tf_op jit(solution)/shard_map/ppermute | solution.py:35
  102.8 7.4 %collective-permute-start.28 = (bf16[1,64,4,32]{1,3,2,0:T(8,128)(2,1)S(1)}, bf16[1,64,4,32]{1,3,2,0:T(8,128)(2,1)S(1)}, u32[]{:S(2)}, u32[]{:S(2)}) collective-permute-start(bf16[1,64,4,32]{1,3,2,0:T(8,128)(2,1)S(1)} %copy.326), channel_id=1, source_target_pairs={{0,20},{2,22},{4,24},{6,26},{8,28},{10,30},{12,0},{14,2},{16,4},{1... | collective-permute-start | bytes 49160 | tf_op jit(solution)/shard_map/ppermute | solution.py:35
  104.1 8.3 %collective-permute-start.29 = (bf16[1,64,4,32]{1,3,2,0:T(8,128)(2,1)S(1)}, bf16[1,64,4,32]{1,3,2,0:T(8,128)(2,1)S(1)}, u32[]{:S(2)}, u32[]{:S(2)}) collective-permute-start(bf16[1,64,4,32]{1,3,2,0:T(8,128)(2,1)S(1)} %copy.327), channel_id=1, source_target_pairs={{0,22},{2,24},{4,26},{6,28},{8,30},{10,0},{12,2},{14,4},{16,6},{18... | collective-permute-start | bytes 49160 | tf_op jit(solution)/shard_map/ppermute | solution.py:35
  112.5 8.5 %collective-permute-start.3 = (bf16[1,64,4,32]{1,3,2,0:T(8,128)(2,1)S(1)}, bf16[1,64,4,32]{1,3,2,0:T(8,128)(2,1)S(1)}, u32[]{:S(2)}, u32[]{:S(2)}) collective-permute-start(bf16[1,64,4,32]{1,3,2,0:T(8,128)(2,1)S(1)} %copy.288), channel_id=1, source_target_pairs={{0,4},{2,6},{4,8},{6,10},{8,12},{10,14},{12,16},{14,18},{16,20},{1... | collective-permute-start | bytes 49160 | tf_op jit(solution)/shard_map/ppermute | solution.py:35
  113.1 11.0 %collective-permute-start.4 = (bf16[1,64,4,32]{1,3,2,0:T(8,128)(2,1)S(1)}, bf16[1,64,4,32]{1,3,2,0:T(8,128)(2,1)S(1)}, u32[]{:S(2)}, u32[]{:S(2)}) collective-permute-start(bf16[1,64,4,32]{1,3,2,0:T(8,128)(2,1)S(1)} %copy.289), channel_id=1, source_target_pairs={{0,6},{2,8},{4,10},{6,12},{8,14},{10,16},{12,18},{14,20},{16,22},{... | collective-permute-start | bytes 49160 | tf_op jit(solution)/shard_map/ppermute | solution.py:35
  114.6 11.4 %collective-permute-start.5 = (bf16[1,64,4,32]{1,3,2,0:T(8,128)(2,1)S(1)}, bf16[1,64,4,32]{1,3,2,0:T(8,128)(2,1)S(1)}, u32[]{:S(2)}, u32[]{:S(2)}) collective-permute-start(bf16[1,64,4,32]{1,3,2,0:T(8,128)(2,1)S(1)} %copy.290), channel_id=1, source_target_pairs={{0,8},{2,10},{4,12},{6,14},{8,16},{10,18},{12,20},{14,22},{16,24},... | collective-permute-start | bytes 49160 | tf_op jit(solution)/shard_map/ppermute | solution.py:35
  115.0 11.1 %collective-permute-start.6 = (bf16[1,64,4,32]{1,3,2,0:T(8,128)(2,1)S(1)}, bf16[1,64,4,32]{1,3,2,0:T(8,128)(2,1)S(1)}, u32[]{:S(2)}, u32[]{:S(2)}) collective-permute-start(bf16[1,64,4,32]{1,3,2,0:T(8,128)(2,1)S(1)} %copy.291), channel_id=1, source_target_pairs={{0,10},{2,12},{4,14},{6,16},{8,18},{10,20},{12,22},{14,24},{16,26}... | collective-permute-start | bytes 49160 | tf_op jit(solution)/shard_map/ppermute | solution.py:35
  119.0 9.2 %collective-permute-start.7 = (bf16[1,64,4,32]{1,3,2,0:T(8,128)(2,1)S(1)}, bf16[1,64,4,32]{1,3,2,0:T(8,128)(2,1)S(1)}, u32[]{:S(2)}, u32[]{:S(2)}) collective-permute-start(bf16[1,64,4,32]{1,3,2,0:T(8,128)(2,1)S(1)} %copy.292), channel_id=1, source_target_pairs={{0,12},{2,14},{4,16},{6,18},{8,20},{10,22},{12,24},{14,26},{16,28}... | collective-permute-start | bytes 49160 | tf_op jit(solution)/shard_map/ppermute | solution.py:35
  120.9 8.9 %collective-permute-start.8 = (bf16[1,64,4,32]{1,3,2,0:T(8,128)(2,1)S(1)}, bf16[1,64,4,32]{1,3,2,0:T(8,128)(2,1)S(1)}, u32[]{:S(2)}, u32[]{:S(2)}) collective-permute-start(bf16[1,64,4,32]{1,3,2,0:T(8,128)(2,1)S(1)} %copy.293), channel_id=1, source_target_pairs={{0,14},{2,16},{4,18},{6,20},{8,22},{10,24},{12,26},{14,28},{16,30}... | collective-permute-start | bytes 49160 | tf_op jit(solution)/shard_map/ppermute | solution.py:35
  124.1 8.0 %collective-permute-start.9 = (bf16[1,64,4,32]{1,3,2,0:T(8,128)(2,1)S(1)}, bf16[1,64,4,32]{1,3,2,0:T(8,128)(2,1)S(1)}, u32[]{:S(2)}, u32[]{:S(2)}) collective-permute-start(bf16[1,64,4,32]{1,3,2,0:T(8,128)(2,1)S(1)} %copy.294), channel_id=1, source_target_pairs={{0,16},{2,18},{4,20},{6,22},{8,24},{10,26},{12,28},{14,30},{16,0},... | collective-permute-start | bytes 49160 | tf_op jit(solution)/shard_map/ppermute | solution.py:35
  126.1 8.5 %collective-permute-start.11 = (bf16[1,64,4,32]{1,3,2,0:T(8,128)(2,1)S(1)}, bf16[1,64,4,32]{1,3,2,0:T(8,128)(2,1)S(1)}, u32[]{:S(2)}, u32[]{:S(2)}) collective-permute-start(bf16[1,64,4,32]{1,3,2,0:T(8,128)(2,1)S(1)} %copy.296), channel_id=1, source_target_pairs={{0,20},{2,22},{4,24},{6,26},{8,28},{10,30},{12,0},{14,2},{16,4},{1... | collective-permute-start | bytes 49160 | tf_op jit(solution)/shard_map/ppermute | solution.py:35
  129.8 7.7 %collective-permute-start.13 = (bf16[1,64,4,32]{1,3,2,0:T(8,128)(2,1)S(1)}, bf16[1,64,4,32]{1,3,2,0:T(8,128)(2,1)S(1)}, u32[]{:S(2)}, u32[]{:S(2)}) collective-permute-start(bf16[1,64,4,32]{1,3,2,0:T(8,128)(2,1)S(1)} %copy.298), channel_id=1, source_target_pairs={{0,24},{2,26},{4,28},{6,30},{8,0},{10,2},{12,4},{14,6},{16,8},{18,... | collective-permute-start | bytes 49160 | tf_op jit(solution)/shard_map/ppermute | solution.py:35
  132.1 7.8 %collective-permute-start.14 = (bf16[1,64,4,32]{1,3,2,0:T(8,128)(2,1)S(1)}, bf16[1,64,4,32]{1,3,2,0:T(8,128)(2,1)S(1)}, u32[]{:S(2)}, u32[]{:S(2)}) collective-permute-start(bf16[1,64,4,32]{1,3,2,0:T(8,128)(2,1)S(1)} %copy.299), channel_id=1, source_target_pairs={{0,26},{2,28},{4,30},{6,0},{8,2},{10,4},{12,6},{14,8},{16,10},{18,... | collective-permute-start | bytes 49160 | tf_op jit(solution)/shard_map/ppermute | solution.py:35
  132.2 7.8 %collective-permute-start.15 = (bf16[1,64,4,32]{1,3,2,0:T(8,128)(2,1)S(1)}, bf16[1,64,4,32]{1,3,2,0:T(8,128)(2,1)S(1)}, u32[]{:S(2)}, u32[]{:S(2)}) collective-permute-start(bf16[1,64,4,32]{1,3,2,0:T(8,128)(2,1)S(1)} %copy.300), channel_id=1, source_target_pairs={{0,28},{2,30},{4,0},{6,2},{8,4},{10,6},{12,8},{14,10},{16,12},{18,... | collective-permute-start | bytes 49160 | tf_op jit(solution)/shard_map/ppermute | solution.py:35
  135.6 11.9 %collective-permute-start.35 = (f32[16,4,32]{0,2,1:T(8,128)S(1)}, f32[16,4,32]{0,2,1:T(8,128)S(1)}, u32[]{:S(2)}, u32[]{:S(2)}) collective-permute-start(f32[16,4,32]{0,2,1:T(8,128)S(1)} %get-tuple-element.189), channel_id=1, source_target_pairs={{2,0},{4,2},{6,4},{8,6},{10,8},{12,10},{14,12},{16,14},{18,16},{20... | collective-permute-start | bytes 24584 | tf_op jit(solution)/shard_map/ppermute | solution.py:56
  137.6 9.9 %collective-permute-start.34 = (f32[16,4,32]{0,2,1:T(8,128)S(1)}, f32[16,4,32]{0,2,1:T(8,128)S(1)}, u32[]{:S(2)}, u32[]{:S(2)}) collective-permute-start(f32[16,4,32]{0,2,1:T(8,128)S(1)} %get-tuple-element.188), channel_id=1, source_target_pairs={{0,2},{2,4},{4,6},{6,8},{8,10},{10,12},{12,14},{14,16},{16,18},{18... | collective-permute-start | bytes 24584 | tf_op jit(solution)/shard_map/ppermute | solution.py:55
  (33 other events, 115.6 us)
